TPU v7x, 256 devices: a whole 4x4x8 slice. The times are simulated.
256 devices in a mesh: dp: 8 (over z_lo, y), expert: 32 (over x, z_hi, core).
Axes of the slice: x: 4, y: 4, z: 8 (z_hi: 4, z_lo: 2; z = z_hi * 2 + z_lo), core: 2. Of those that a mesh axis runs over, the one named last changes fastest.
Arguments:
- x_tokens: bfloat16 [32768, 2048], P(('dp', 'expert')), may hold values from -6 to 6
- dy_tokens: bfloat16 [32768, 2048], P(('dp', 'expert')), may hold values from -24 to 24
- probs: bfloat16 [32768, 8], P(('dp', 'expert')), may hold values from 0.049804688 to 0.5
- ids: int32 [32768, 8], P(('dp', 'expert')), may hold values from 0 to 127, all different within a row
- w_gate: bfloat16 [32, 2048, 768], P('expert'), may hold values from -0.125 to 0.125
- w_up: bfloat16 [32, 2048, 768], P('expert'), may hold values from -0.125 to 0.125
- w_down: bfloat16 [32, 2048, 768], P('expert'), may hold values from -0.21875 to 0.21875
Outputs:
- x_grad: bfloat16 [32768, 2048], P(('dp', 'expert'))
- gate_grad: float32 [32, 2048, 768], P('expert', 'dp')
- up_grad: float32 [32, 2048, 768], P('expert', 'dp')
- down_grad: float32 [32, 2048, 768], P('expert', 'dp')
Inputs may be any that keep to these rules, and one draw needn't show every extreme that they name: `ids`: each row names 8 different experts.
All inputs are finite; a program needn't handle non-finite values.
Results may differ from a plain program's by a relative error of at most 0.0063.
Values may be sent and summed in bfloat16 or wider, within the bound.
A program may use at most 128 MiB of HBM per device.

v0:
```python
import jax
import jax.numpy as jnp
from jax import lax
from jax.sharding import PartitionSpec as P

CAP = 10


def expert_pass(expert_rows, out_grads, gate_scale, gate_mat, up_mat, down_mat):
    gate_pre = jnp.dot(expert_rows, gate_mat, preferred_element_type=jnp.float32)
    up_pre = jnp.dot(expert_rows, up_mat, preferred_element_type=jnp.float32)
    gate_sig = jax.nn.sigmoid(gate_pre)
    gate_act = gate_pre * gate_sig
    hidden = (gate_act * up_pre).astype(jnp.bfloat16)
    scaled = (gate_scale[:, None].astype(jnp.float32) * out_grads.astype(jnp.float32)).astype(
        jnp.bfloat16
    )
    hidden_grad = jnp.dot(scaled, down_mat, preferred_element_type=jnp.float32)
    up_delta = (hidden_grad * gate_act).astype(jnp.bfloat16)
    gate_delta = (hidden_grad * up_pre * gate_sig * (1.0 + gate_pre * (1.0 - gate_sig))).astype(
        jnp.bfloat16
    )
    dims = (((1,), (1,)), ((), ()))
    slot_back = lax.dot_general(gate_delta, gate_mat, dims, preferred_element_type=jnp.float32)
    slot_back = slot_back + lax.dot_general(
        up_delta, up_mat, dims, preferred_element_type=jnp.float32
    )
    return (hidden, scaled, gate_delta, up_delta, slot_back.astype(jnp.bfloat16))


def rows_product(left_rows, right_rows):
    return lax.dot_general(
        left_rows, right_rows, (((0,), (0,)), ((), ())), preferred_element_type=jnp.float32
    )


def on_device(x_tokens, dy_tokens, probs, ids, w_gate, w_up, w_down):
    num_experts = lax.axis_size("expert")
    tok_rows = x_tokens.shape[0]
    model_width = x_tokens.shape[1]
    top_k = ids.shape[1]
    hidden_width = w_gate.shape[2]
    per_block = tok_rows * top_k
    slot_count = num_experts * CAP
    flat_ids = ids.reshape(per_block)
    onehot = (flat_ids[:, None] == jnp.arange(num_experts, dtype=jnp.int32)[None, :]).astype(
        jnp.int32
    )
    slot_rank = jnp.sum((jnp.cumsum(onehot, axis=0) - onehot) * onehot, axis=1)
    kept_mask = (flat_ids < num_experts) & (slot_rank < CAP)
    target = jnp.where(kept_mask, flat_ids * CAP + slot_rank, -1)
    slot_match = target[None, :] == jnp.arange(slot_count, dtype=jnp.int32)[:, None]
    pick_rows = jnp.any(slot_match.reshape(slot_count, tok_rows, top_k), axis=2).astype(
        jnp.bfloat16
    )
    x_send = jnp.dot(pick_rows, x_tokens, preferred_element_type=jnp.float32).astype(jnp.bfloat16)
    dy_send = jnp.dot(pick_rows, dy_tokens, preferred_element_type=jnp.float32).astype(jnp.bfloat16)
    prob_row = probs.reshape(1, per_block).astype(jnp.float32)
    p_send = jnp.sum(jnp.where(slot_match, prob_row, 0.0), axis=1).astype(jnp.bfloat16)
    expert_rows, out_grads, gate_scale = (
        lax.all_to_all(
            x_send.reshape(num_experts, CAP, model_width),
            "expert",
            split_axis=0,
            concat_axis=0,
            tiled=True,
        ),
        lax.all_to_all(
            dy_send.reshape(num_experts, CAP, model_width),
            "expert",
            split_axis=0,
            concat_axis=0,
            tiled=True,
        ),
        lax.all_to_all(
            p_send.reshape(num_experts, CAP), "expert", split_axis=0, concat_axis=0, tiled=True
        ),
    )
    expert_rows = expert_rows.reshape(slot_count, model_width)
    out_grads = out_grads.reshape(slot_count, model_width)
    gate_scale = gate_scale.reshape(slot_count)
    hidden, scaled, gate_delta, up_delta, slot_back = expert_pass(
        expert_rows, out_grads, gate_scale, w_gate[0], w_up[0], w_down[0]
    )
    returned = lax.all_to_all(
        slot_back.reshape(num_experts, CAP, model_width),
        "expert",
        split_axis=0,
        concat_axis=0,
        tiled=True,
    )
    x_grad = rows_product(pick_rows, returned.reshape(slot_count, model_width)).astype(jnp.bfloat16)
    stacked = lax.psum_scatter(
        jnp.concatenate(
            [
                rows_product(expert_rows, gate_delta),
                rows_product(expert_rows, up_delta),
                rows_product(scaled, hidden),
            ],
            axis=1,
        ),
        "dp",
        scatter_dimension=0,
        tiled=True,
    )
    gate_grad = stacked[:, :hidden_width][None]
    up_grad = stacked[:, hidden_width : 2 * hidden_width][None]
    down_grad = stacked[:, 2 * hidden_width :][None]
    return (x_grad, gate_grad, up_grad, down_grad)


def solution(mesh):
    placed = (
        P(("dp", "expert"), None),
        P(("dp", "expert"), None),
        P(("dp", "expert"), None),
        P(("dp", "expert"), None),
        P("expert", None, None),
        P("expert", None, None),
        P("expert", None, None),
    )
    return jax.shard_map(
        on_device,
        mesh=mesh,
        in_specs=placed,
        out_specs=(
            P(("dp", "expert"), None),
            P("expert", "dp", None),
            P("expert", "dp", None),
            P("expert", "dp", None),
        ),
        check_vma=False,
    )
```

profile of v0, /device:TPU:1, one launch (start us, length us, event | category | flops | bytes accessed | tf_op | source)
XLA Modules:
  0.0 446.8 jit_solution(1904023286449162517)
XLA Ops:
  9.2 9.0 %reduce-window.6 = s32[32,8,128]{2,1,0:T(8,128)S(1)} reduce-window(s32[32,8,128]{2,1,0:T(8,128)S(1)} %fusion.24, s32[]{:T(128)} %constant.3.clone.1), window={size=1x1x128 pad=0_0x0_0x127_0}, to_apply=%region_0.0 | reduce-window | flops 4161536 | bytes 262148 | tf_op jit(solution)/shard_map/reduce-window
  19.7 12.6 %all-to-all-start = ((bf16[32,1,10]{2,1,0:T(2,128)(2,1)}), bf16[32,1,10]{2,1,0:T(2,128)(2,1)S(1)}, u32[]{:S(2)}, u32[]{:S(2)}) async-start(bf16[32,1,10]{2,1,0:T(2,128)(2,1)} %convert_element_type.115), calls=%async_computation | async-start | bytes 32768 | tf_op jit(solution)/shard_map/all_to_all | solution.py:75
  36.2 3.3 reshape.115
  41.6 7.8 %all-to-all-start.2 = ((bf16[32,10,2048]{2,1,0:T(8,128)(2,1)}), bf16[32,10,2048]{2,1,0:T(8,128)(2,1)}, u32[]{:S(2)}, u32[]{:S(2)}) async-start(bf16[32,10,2048]{2,1,0:T(8,128)(2,1)} %reshape.115), calls=%async_computation.2 | async-start | bytes 4194304 | tf_op jit(solution)/shard_map/all_to_all | solution.py:61
  49.4 2.6 convolution_convert_fusion.1
  52.0 3.3 reshape.114
  55.4 44.1 %all-to-all-done.2 = bf16[32,10,2048]{2,1,0:T(8,128)(2,1)} async-done(((bf16[32,10,2048]{2,1,0:T(8,128)(2,1)}), bf16[32,10,2048]{2,1,0:T(8,128)(2,1)}, u32[]{:S(2)}, u32[]{:S(2)}) %all-to-all-start.2) | async-done | bytes 1310752 | tf_op jit(solution)/shard_map/all_to_all | solution.py:61
  99.4 5.8 %all-to-all-start.1 = ((bf16[32,10,2048]{2,1,0:T(8,128)(2,1)}), bf16[32,10,2048]{2,1,0:T(8,128)(2,1)}, u32[]{:S(2)}, u32[]{:S(2)}) async-start(bf16[32,10,2048]{2,1,0:T(8,128)(2,1)} %reshape.114), calls=%async_computation.1 | async-start | bytes 4194304 | tf_op jit(solution)/shard_map/all_to_all | solution.py:68
  105.4 3.8 reshape.116
  109.2 3.6 fusion.2
  115.0 30.5 %all-to-all-done.1 = bf16[32,10,2048]{2,1,0:T(8,128)(2,1)} async-done(((bf16[32,10,2048]{2,1,0:T(8,128)(2,1)}), bf16[32,10,2048]{2,1,0:T(8,128)(2,1)}, u32[]{:S(2)}, u32[]{:S(2)}) %all-to-all-start.1) | async-done | bytes 1310752 | tf_op jit(solution)/shard_map/all_to_all | solution.py:68
  145.5 3.4 multiply_convert_fusion
  148.8 3.6 convert_element_type.99
  152.4 4.3 multiply_convert_fusion.4
  156.7 4.4 fusion.27
  161.2 4.5 %fusion.26 = f32[2048,768]{0,1:T(8,128)} fusion(bf16[320,2048]{1,0:T(8,128)(2,1)S(1)} %copy-done.3, bf16[320,768]{1,0:T(8,128)(2,1)S(1)} %get-tuple-element.28), kind=kOutput, calls=%fused_computation.44 | convolution fusion | flops 1006632960 | bytes 8093696 | tf_op jit(solution)/shard_map/dot_general | solution.py:32
  165.7 3.7 reshape.122
  169.5 4.4 fusion.16
  173.9 9.5 %pad_maximum_fusion = f32[2048,2304]{0,1:T(8,128)} fusion(f32[2048,768]{0,1:T(8,128)S(1)} %fusion.16, f32[2048,768]{0,1:T(8,128)} %fusion.27, f32[2048,768]{0,1:T(8,128)S(1)} %copy-done.1), kind=kLoop, calls=%fused_computation | loop fusion | flops 9437184 | bytes 37748736 | tf_op jit(solution)/shard_map/concatenate | solution.py:94
  188.1 3.3 reshape.117
  191.4 90.1 %all_to_all.21 = bf16[32,10,2048]{2,1,0:T(8,128)(2,1)} all-to-all(bf16[32,10,2048]{2,1,0:T(8,128)(2,1)} %reshape.117), channel_id=1, replica_groups=mesh['dp'=8,'expert'=32] {'expert'}, dimensions={0} | all-to-all | bytes 2621440 | tf_op jit(solution)/shard_map/all_to_all | solution.py:85
  281.5 3.6 reshape.118
  287.7 142.4 %reduce-scatter.2.cloned.1.call-done = f32[256,2304]{0,1:T(8,128)} async-done(((f32[2048,2304]{0,1:T(8,128)}), f32[256,2304]{0,1:T(8,128)}) %reduce-scatter.2.cloned.1.call-update) | async-done | bytes 2359312 | tf_op jit(solution)/shard_map/reduce_scatter | solution.py:93
  430.1 3.1 slice_bitcast_fusion
  (52 shorter events, 26.0 us)
Async XLA Ops:
  7.2 102.1 %copy-start = (bf16[1,2048,768]{2,1,0:T(8,128)(2,1)S(1)}, bf16[1,2048,768]{2,1,0:T(8,128)(2,1)}, u32[]{:S(2)}) copy-start(bf16[1,2048,768]{2,1,0:T(8,128)(2,1)} %param.11) | copy-start | bytes 9437188
  19.7 21.9 %all-to-all-start = ((bf16[32,1,10]{2,1,0:T(2,128)(2,1)}), bf16[32,1,10]{2,1,0:T(2,128)(2,1)S(1)}, u32[]{:S(2)}, u32[]{:S(2)}) async-start(bf16[32,1,10]{2,1,0:T(2,128)(2,1)} %convert_element_type.115), calls=%async_computation | async-start | bytes 32768 | tf_op jit(solution)/shard_map/all_to_all | solution.py:75
  41.6 57.8 %all-to-all-start.2 = ((bf16[32,10,2048]{2,1,0:T(8,128)(2,1)}), bf16[32,10,2048]{2,1,0:T(8,128)(2,1)}, u32[]{:S(2)}, u32[]{:S(2)}) async-start(bf16[32,10,2048]{2,1,0:T(8,128)(2,1)} %reshape.115), calls=%async_computation.2 | async-start | bytes 4194304 | tf_op jit(solution)/shard_map/all_to_all | solution.py:61
  99.4 46.1 %all-to-all-start.1 = ((bf16[32,10,2048]{2,1,0:T(8,128)(2,1)}), bf16[32,10,2048]{2,1,0:T(8,128)(2,1)}, u32[]{:S(2)}, u32[]{:S(2)}) async-start(bf16[32,10,2048]{2,1,0:T(8,128)(2,1)} %reshape.114), calls=%async_computation.1 | async-start | bytes 4194304 | tf_op jit(solution)/shard_map/all_to_all | solution.py:68
  105.2 324.9 %reduce-scatter.2.cloned.1.call-start = ((), (), s32[]{:S(2)}) async-start(), calls=%async_computation.5 | async-start | bytes 21233664 | tf_op jit(solution)/shard_map/reduce_scatter | solution.py:93
  109.2 3.6 copy-start.2
  109.2 3.6 copy-start.7
  152.4 4.3 copy-start.3
  156.7 4.5 %copy-start.4 = (bf16[320,768]{1,0:T(8,128)(2,1)}, bf16[320,768]{1,0:T(8,128)(2,1)S(1)}, u32[]{:S(2)}) copy-start(bf16[320,768]{1,0:T(8,128)(2,1)S(1)} %get-tuple-element.27) | copy-start | bytes 1474564
  156.7 4.5 %copy-start.6 = (bf16[320,768]{1,0:T(8,128)(2,1)}, bf16[320,768]{1,0:T(8,128)(2,1)S(1)}, u32[]{:S(2)}) copy-start(bf16[320,768]{1,0:T(8,128)(2,1)S(1)} %get-tuple-element.28) | copy-start | bytes 1474564
  169.5 4.4 copy-start.1
  183.4 2.4 copy-start.5
  183.4 2.4 copy-start.8
Sparse Core Ops, SparseCore 0:
  183.5 246.5 reduce-scatter.1
where the time goes:
time: 448 us; the launch traced here: 447 us
  waiting for transfers between devices  219 us (49%)
  blocking collectives  90.1 us (20%)
  local copies, waits for them, and re-layouts  37.9 us (8%)
  matrix products  35.9 us (8%)
  starting transfers between devices  26.2 us (6%)
  other arithmetic  23.5 us (5%)
  between operations  14.2 us (3%)
    reduce_scatter x1, waiting for transfers between devices, on_device(): lax.psum_scatter(jnp.concatenate([rows_product(expert_rows, gate_delta),...  142 us
    all_to_all x1, blocking collectives, on_device(): lax.all_to_all(slot_back.reshape(num_experts, CAP, model_width), 'expert'...  90.1 us
    all_to_all x1, waiting for transfers between devices, on_device(): lax.all_to_all(x_send.reshape(num_experts, CAP, model_width), 'expert', s...  44.1 us
    all_to_all x1, waiting for transfers between devices, on_device(): lax.all_to_all(dy_send.reshape(num_experts, CAP, model_width), 'expert',...  30.5 us
    dot_general x4, matrix products, rows_product(): lax.dot_general(left_rows, right_rows, (((0,), (0,)), ((), ())), preferre...  15.9 us
    all_to_all x1, starting transfers between devices, on_device(): lax.all_to_all(p_send.reshape(num_experts, CAP), 'expert', split_axis=0,...  12.6 us
    concatenate x1, other arithmetic, on_device(): jnp.concatenate([rows_product(expert_rows, gate_delta), rows_product(expe...  9.49 us
    another operation x3, other arithmetic  9.15 us
  transfers between devices with their start and end apart: 4, of which 4 were waited for; matrix products, arithmetic and copies ran while one was open for 8% of the time, Pallas kernels for 0%

commit v1 on v0

v1 whole, which is shorter than its diff:
```python
import functools

import jax
import jax.numpy as jnp
import numpy as np
from jax import lax
from jax.experimental import pallas as pl
from jax.experimental.pallas import tpu as pltpu
from jax.sharding import PartitionSpec as P

MESH = pl.DeviceIdType.MESH
F32, BF16 = jnp.float32, jnp.bfloat16
CAP = 10
TOK = 128
D = 2048
HW = 768
NX = 4
ZC = 8
NY = 4
CB = 8
CW = D // CB
ROWS = ZC * CAP
CHUNK = CB * CAP
GROUP = ZC * CHUNK
SLOTS = NX * ROWS
HALF = 2 * ROWS


def dot(a, b, ca=1, cb=0):
    return lax.dot_general(a, b, (((ca,), (cb,)), ((), ())), preferred_element_type=F32)


def kernel(
    ids_ref, p_ref, tgt_ref, inv_ref, x_ref, dy_ref, wg_hbm, wu_hbm, wd_hbm,
    xg_ref, gg_ref, ug_ref, dg_ref,
    wgu, wd, pick, pickp, toa, tos,
    s_x, r_x, s_s, r_s, s_b, r_b, a_x, a_s, a_b,
    act, gfac, hid, gu, xs, ss, dh, dgu, z_s, z_r,
    wsem, lsem, sx_sem, rx_sem, sd_sem, rd_sem, sb_sem, rb_sem,
    yx_s, yx_r, ys_s, ys_r, yh_s, yh_r, yg_s, yg_r, zz_s, zz_r,
):
    dpi = lax.axis_index("dp")
    me = lax.axis_index("expert")
    zl, y = dpi // NY, lax.rem(dpi, NY)
    xi, zc = me // ZC, lax.rem(me, ZC)

    loads = [
        pltpu.make_async_copy(wg_hbm.at[0], wgu.at[:, pl.ds(0, HW)], wsem.at[0]),
        pltpu.make_async_copy(wu_hbm.at[0], wgu.at[:, pl.ds(HW, HW)], wsem.at[1]),
        pltpu.make_async_copy(wd_hbm.at[0], wd, wsem.at[2]),
    ]
    for load in loads:
        load.start()

    barrier = pltpu.get_barrier_semaphore()
    for k in range(1, NX * ZC):
        pl.semaphore_signal(
            barrier, inc=1, device_id=(dpi, lax.rem(me + k, NX * ZC)), device_id_type=MESH
        )
    for k in range(1, NY):
        pl.semaphore_signal(
            barrier, inc=1, device_id=(zl * NY + lax.rem(y + k, NY), me), device_id_type=MESH
        )
    partner = (1 - zl) * NY + y
    pl.semaphore_signal(barrier, inc=1, device_id=(partner, me), device_id_type=MESH)

    row = lax.broadcasted_iota(jnp.int32, (NX * ZC, TOK), 0)
    expert = row + ZC * xi
    expert = jnp.where(expert >= NX * ZC, expert - NX * ZC, expert)
    member = jnp.zeros((NX * ZC, TOK), F32)
    weight = jnp.zeros((NX * ZC, TOK), F32)
    probs = p_ref[...].astype(F32)
    for k in range(8):
        same = ids_ref[k : k + 1, :] == expert
        member = jnp.where(same, 1.0, member)
        weight = jnp.where(same, probs[k : k + 1, :], weight)
    before = lax.broadcasted_iota(jnp.int32, (TOK, TOK), 0) < lax.broadcasted_iota(
        jnp.int32, (TOK, TOK), 1
    )
    rank = dot(member.astype(BF16), jnp.where(before, 1.0, 0.0).astype(BF16))
    rank = jnp.where(member > 0.5, rank, -1.0).astype(BF16)
    slot = lax.broadcasted_iota(jnp.int32, (SLOTS, NX * ZC), 0)
    first = CAP * lax.broadcasted_iota(jnp.int32, (SLOTS, NX * ZC), 1)
    spread = jnp.where((slot >= first) & (slot < first + CAP), 1.0, 0.0).astype(BF16)
    of_rank = dot(spread, rank)
    of_weight = dot(spread, weight.astype(BF16))
    of_row = dot(spread, row.astype(F32).astype(BF16))
    place = lax.broadcasted_iota(jnp.int32, (SLOTS, TOK), 0).astype(F32) - CAP * of_row
    hit = of_rank == place
    pick[...] = jnp.where(hit, 1.0, 0.0).astype(BF16)
    pickp[...] = jnp.where(hit, of_weight, 0.0).astype(BF16)
    down = lax.broadcasted_iota(jnp.int32, (GROUP, GROUP), 0)
    tos[...] = jnp.where(down == tgt_ref[...], 1.0, 0.0).astype(BF16)
    toa[...] = jnp.where(down == inv_ref[...], 1.0, 0.0).astype(BF16)

    def exchange(src, dst, send, recv, j, i, sign):
        zt = lax.rem(zc + i, ZC)
        xt = lax.rem(xi + sign * j + NX, NX)
        from_rows = pl.ds(pl.multiple_of((j * ZC + zt) * CHUNK, 16), CHUNK)
        to_rows = pl.ds(pl.multiple_of((j * ZC + zc) * CHUNK, 16), CHUNK)
        if i == 0 and j == 0:
            return pltpu.make_async_copy(src.at[from_rows], dst.at[to_rows], recv.at[0])
        return pltpu.make_async_remote_copy(
            src_ref=src.at[from_rows],
            dst_ref=dst.at[to_rows],
            send_sem=send.at[j * ZC + i],
            recv_sem=recv.at[j * ZC + i],
            device_id=(dpi, xt * ZC + zt),
            device_id_type=MESH,
        )

    sent = []

    def start_group(src, dst, send, recv, j, sign):
        for i in range(ZC):
            copy = exchange(src, dst, send, recv, j, i, sign)
            copy.start()
            if i or j:
                sent.append(copy)

    def wait_group(src, dst, send, recv, j, sign):
        for i in range(ZC):
            copy = exchange(src, dst, send, recv, j, i, sign)
            if i or j:
                copy.wait_recv()
            else:
                copy.wait()

    def pack(blocks):
        return dot(tos[...], jnp.concatenate(blocks, axis=0)).astype(BF16)

    def unpack(src, dst, j):
        rows = dot(toa[...], src[j * GROUP : (j + 1) * GROUP, :]).astype(BF16)
        for c in range(CB):
            dst[c, j * ROWS : (j + 1) * ROWS, :] = rows[c * ROWS : (c + 1) * ROWS, :]

    def gather(sel, tokens, dst, j):
        rows = dot(sel[j * ROWS : (j + 1) * ROWS, :], tokens[...]).astype(BF16)
        dst[j * GROUP : (j + 1) * GROUP, :] = pack(
            [rows[:, c * CW : (c + 1) * CW] for c in range(CB)]
        )

    for j in range(NX):
        gather(pick, x_ref, s_x, j)
        if j == 0:
            pl.semaphore_wait(barrier, NX * ZC - 1 + NY)
        start_group(s_x, r_x, sx_sem, rx_sem, j, 1)
    for j in range(NX):
        gather(pickp, dy_ref, s_s, j)
        start_group(s_s, r_s, sd_sem, rd_sem, j, 1)

    def to_y(src, dst, send, recv, k):
        return pltpu.make_async_remote_copy(
            src_ref=src,
            dst_ref=dst,
            send_sem=send,
            recv_sem=recv,
            device_id=(zl * NY + lax.rem(y + k, NY), me),
            device_id_type=MESH,
        )

    def slice_copy(src, dst, send, recv, k, b, h):
        part = pl.ds(h * HALF, HALF)
        n = (k * 2 + b) * 2 + h
        yt = lax.rem(y + k, NY)
        return to_y(
            src.at[b * NY + yt, part], dst.at[k, b, part], send.at[n], recv.at[n], k
        )

    def start_slices(src, dst, send, recv, h):
        for k in range(1, NY):
            for b in range(2):
                copy = slice_copy(src, dst, send, recv, k, b, h)
                copy.start()
                sent.append(copy)

    def wait_slices(src, dst, send, recv):
        for h in range(2):
            for k in range(1, NY):
                for b in range(2):
                    slice_copy(src, dst, send, recv, k, b, h).wait_recv()

    for h in range(2):
        for j in (2 * h, 2 * h + 1):
            wait_group(s_x, r_x, sx_sem, rx_sem, j, 1)
            unpack(r_x, a_x, j)
        start_slices(a_x, xs, yx_s, yx_r, h)

    for load in loads:
        load.wait()
    for h in range(2):
        part = slice(h * HALF, (h + 1) * HALF)
        rows = jnp.concatenate([a_x[c, part, :] for c in range(CB)], axis=1)
        for n in range(HW // CW):
            cols = slice(n * CW, (n + 1) * CW)
            gate_pre = dot(rows, wgu[:, n * CW : (n + 1) * CW])
            up_pre = dot(rows, wgu[:, HW + n * CW : HW + (n + 1) * CW])
            sig = 1.0 / (1.0 + jnp.exp(-gate_pre))
            gate_act = gate_pre * sig
            act[part, cols] = gate_act
            gfac[part, cols] = up_pre * sig * (1.0 + gate_pre * (1.0 - sig))
            hid[part, cols] = (gate_act * up_pre).astype(BF16)

    def hid_copy(k):
        return to_y(hid, dh.at[k], yh_s.at[k], yh_r.at[k], k)

    def gu_copy(k, h):
        part = pl.ds(h * HALF, HALF)
        return to_y(gu.at[part], dgu.at[k, part], yg_s.at[2 * k + h], yg_r.at[2 * k + h], k)

    for k in range(1, NY):
        hid_copy(k).start()
        sent.append(hid_copy(k))

    for h in range(2):
        part = slice(h * HALF, (h + 1) * HALF)
        for j in (2 * h, 2 * h + 1):
            wait_group(s_s, r_s, sd_sem, rd_sem, j, 1)
            unpack(r_s, a_s, j)
        start_slices(a_s, ss, ys_s, ys_r, h)
        rows = jnp.concatenate([a_s[c, part, :] for c in range(CB)], axis=1)
        for n in range(HW // CW):
            cols = slice(n * CW, (n + 1) * CW)
            hidden_grad = dot(rows, wd[:, n * CW : (n + 1) * CW])
            gu[part, cols] = (hidden_grad * gfac[part, cols]).astype(BF16)
            gu[part, HW + n * CW : HW + (n + 1) * CW] = (hidden_grad * act[part, cols]).astype(BF16)
        for k in range(1, NY):
            gu_copy(k, h).start()
            sent.append(gu_copy(k, h))
        deltas = gu[part, :]
        back = [
            dot(deltas, wgu[c * CW : (c + 1) * CW, :], 1, 1).astype(BF16) for c in range(CB)
        ]
        for g in range(2):
            j = 2 * h + g
            s_b[j * GROUP : (j + 1) * GROUP, :] = pack(
                [block[g * ROWS : (g + 1) * ROWS, :] for block in back]
            )
            start_group(s_b, r_b, sb_sem, rb_sem, j, -1)

    def z_copy(n):
        return pltpu.make_async_remote_copy(
            src_ref=z_s.at[n],
            dst_ref=z_r.at[n],
            send_sem=zz_s.at[n],
            recv_sem=zz_r.at[n],
            device_id=(partner, me),
            device_id_type=MESH,
        )

    def sums(slices, own, b, right):
        total = dot(own[b * NY + y], right(0), 0, 0)
        for k in range(1, NY):
            total = total + dot(slices[k, b], right(k), 0, 0)
        return total

    outs = (gg_ref, ug_ref, dg_ref)
    wait_slices(a_s, ss, ys_s, ys_r)
    for k in range(1, NY):
        hid_copy(k).wait_recv()

    def hid_of(k):
        return hid[...] if k == 0 else dh[k]

    z_s[2] = sums(ss, a_s, 1 - zl, hid_of).astype(BF16)
    z_copy(2).start()
    sent.append(z_copy(2))
    dg_ref[...] = sums(ss, a_s, zl, hid_of)

    wait_slices(a_x, xs, yx_s, yx_r)
    for h in range(2):
        for k in range(1, NY):
            gu_copy(k, h).wait_recv()
    for n in range(2):

        def gu_of(k):
            cols = slice(n * HW, (n + 1) * HW)
            return gu[:, cols] if k == 0 else dgu[k, :, cols]

        z_s[n] = sums(xs, a_x, 1 - zl, gu_of).astype(BF16)
        z_copy(n).start()
        sent.append(z_copy(n))
    for n in range(2):

        def gu_of(k):
            cols = slice(n * HW, (n + 1) * HW)
            return gu[:, cols] if k == 0 else dgu[k, :, cols]

        outs[n][...] = sums(xs, a_x, zl, gu_of)

    for j in range(NX):
        wait_group(s_b, r_b, sb_sem, rb_sem, j, -1)
        unpack(r_b, a_b, j)
    for c in range(CB):
        xg_ref[:, c * CW : (c + 1) * CW] = dot(pick[...], a_b[c], 0, 0).astype(BF16)
    for n in (2, 0, 1):
        z_copy(n).wait_recv()
        outs[n][...] += z_r[n].astype(F32)
    for copy in sent:
        copy.wait_send()


def on_device(x_tokens, dy_tokens, probs, ids, w_gate, w_up, w_down):
    r = np.arange(GROUP)
    c, rest = r // ROWS, r % ROWS
    tgt = (rest // CAP) * CHUNK + c * CAP + rest % CAP
    inv = np.argsort(tgt)
    vmem = pl.BlockSpec(memory_space=pltpu.VMEM)
    anywhere = pl.BlockSpec(memory_space=pl.ANY)
    dma = pltpu.SemaphoreType.DMA
    grad = jax.ShapeDtypeStruct((D // 8, HW), F32)
    chunks = pltpu.VMEM((NX * GROUP, CW), BF16)
    slots = pltpu.VMEM((CB, SLOTS, CW), BF16)
    x_grad, gate_grad, up_grad, down_grad = pl.pallas_call(
        kernel,
        out_shape=(jax.ShapeDtypeStruct((TOK, D), BF16), grad, grad, grad),
        in_specs=[vmem] * 6 + [anywhere] * 3,
        out_specs=[vmem] * 4,
        scratch_shapes=[
            pltpu.VMEM((D, 2 * HW), BF16),
            pltpu.VMEM((D, HW), BF16),
            pltpu.VMEM((SLOTS, TOK), BF16),
            pltpu.VMEM((SLOTS, TOK), BF16),
            pltpu.VMEM((GROUP, GROUP), BF16),
            pltpu.VMEM((GROUP, GROUP), BF16),
        ]
        + [chunks] * 6
        + [slots] * 3
        + [
            pltpu.VMEM((SLOTS, HW), F32),
            pltpu.VMEM((SLOTS, HW), F32),
            pltpu.VMEM((SLOTS, HW), BF16),
            pltpu.VMEM((SLOTS, 2 * HW), BF16),
            pltpu.VMEM((NY, 2, SLOTS, CW), BF16),
            pltpu.VMEM((NY, 2, SLOTS, CW), BF16),
            pltpu.VMEM((NY, SLOTS, HW), BF16),
            pltpu.VMEM((NY, SLOTS, 2 * HW), BF16),
            pltpu.VMEM((3, D // 8, HW), BF16),
            pltpu.VMEM((3, D // 8, HW), BF16),
            dma((3,)),
            dma((1,)),
        ]
        + [dma((NX * ZC,))] * 6
        + [dma((4 * NY,))] * 4
        + [dma((NY,))] * 2
        + [dma((2 * NY,))] * 2
        + [dma((3,))] * 2,
        compiler_params=pltpu.CompilerParams(
            collective_id=0, has_side_effects=True, vmem_limit_bytes=60 << 20
        ),
    )(
        ids.T,
        probs.T,
        jnp.asarray(tgt, jnp.int32)[None],
        jnp.asarray(inv, jnp.int32)[None],
        x_tokens,
        dy_tokens,
        w_gate,
        w_up,
        w_down,
    )
    return (x_grad, gate_grad[None], up_grad[None], down_grad[None])


def solution(mesh):
    rows = P(("dp", "expert"), None)
    held = P("expert", None, None)
    owned = P("expert", "dp", None)
    return jax.shard_map(
        on_device,
        mesh=mesh,
        in_specs=(rows, rows, rows, rows, held, held, held),
        out_specs=(rows, owned, owned, owned),
        check_vma=False,
    )
```

time: 448 us -> 163 us (0.36)
  waiting for transfers between devices: 219 us -> 0 us
  Pallas kernels: 0 us -> 156 us
  blocking collectives: 90.1 us -> 0 us
  matrix products: 35.9 us -> 0 us
  local copies, waits for them, and re-layouts: 37.9 us -> 5.83 us
  starting transfers between devices: 26.2 us -> 0 us
  other arithmetic: 23.5 us -> 0 us
  between operations: 14.2 us -> 0.66 us
    pallas_call x0 -> x1, Pallas kernels: none -> 156 us  [on_device(): pl.pallas_call(kernel, out_shape=(jax.ShapeDtypeStruct((TOK, D), BF16), g...]
    reduce_scatter x1 -> x0, waiting for transfers between devices: 142 us -> none  [on_device(): lax.psum_scatter(jnp.concatenate([rows_product(expert_rows, gate_delta),...]
    all_to_all x1 -> x0, blocking collectives: 90.1 us -> none  [on_device(): lax.all_to_all(slot_back.reshape(num_experts, CAP, model_width), 'expert'...]
    all_to_all x3 -> x0, waiting for transfers between devices: 76.6 us -> none  [the longest x1 44.1 us: on_device(): lax.all_to_all(x_send.reshape(num_experts, CAP, model_width), 'expert', s...]
    dot_general x11 -> x0, matrix products: 35.9 us -> none  [the longest x4 15.9 us: rows_product(): lax.dot_general(left_rows, right_rows, (((0,), (0,)), ((), ())), preferre...]
    all_to_all x3 -> x0, starting transfers between devices: 26.1 us -> none  [the longest x1 12.6 us: on_device(): lax.all_to_all(p_send.reshape(num_experts, CAP), 'expert', split_axis=0,...]
    reshape x5 -> x0, local copies, waits for them, and re-layouts: 17.4 us -> none  [the longest x1 3.78 us: on_device(): expert_rows = expert_rows.reshape(slot_count, model_width)]
    concatenate x1 -> x0, other arithmetic: 9.49 us -> none  [on_device(): jnp.concatenate([rows_product(expert_rows, gate_delta), rows_product(expe...]
  transfers between devices with their start and end apart: 4 -> 0, of which waited for: 4 -> 0; matrix products, arithmetic and copies ran while one was open for 8% -> 0% of each run, Pallas kernels for 0% -> 0%
where the time goes in v1:
time: 163 us; the launch traced here: 162 us
  Pallas kernels  156 us (96%)
  local copies, waits for them, and re-layouts  5.83 us (4%)
    pallas_call x1, Pallas kernels, on_device(): pl.pallas_call(kernel, out_shape=(jax.ShapeDtypeStruct((TOK, D), BF16), g...  156 us
    unnamed x8, local copies, waits for them, and re-layouts  5.83 us

profile of v1, /device:TPU:1, one launch (start us, length us, event | category | flops | bytes accessed | tf_op | source)
XLA Modules:
  0.0 162.3 jit_solution(14325114810453094636)
XLA Ops:
  0.6 155.8 %shard_map.120 = (bf16[128,2048]{1,0:T(8,128)(2,1)}, f32[256,768]{1,0:T(8,128)}, f32[256,768]{1,0:T(8,128)}, f32[256,768]{1,0:T(8,128)}) custom-call(s32[8,128]{1,0:T(8,128)} %bitcast.8, bf16[8,128]{1,0:T(8,128)(2,1)} %bitcast.9, s32[1,640]{1,0:T(1,128)} %constant.10.tgt_ref.inv_ref, s32[1,640]{1,0:T(1,128)} %constant.10.tgt_ref.inv_ref, ...), custom_call_target="tpu_custom_call" | custom-call | tf_op jit(solution)/shard_map/pallas_call | solution.py:314
  156.5 0.0 copy-start.1
  156.5 0.0 copy-start
  156.5 2.0 %copy.17 = bf16[128,2048]{1,0:T(8,128)(2,1)} copy(bf16[128,2048]{1,0:T(8,128)(2,1)} %get-tuple-element.16) | data formatting | bytes 1048576
  158.5 2.1 %copy.18 = f32[1,256,768]{2,1,0:T(8,128)} copy(f32[1,256,768]{2,1,0:T(8,128)} %bitcast.7) | data formatting | bytes 1572864
  160.5 0.0 copy-done.1
  160.5 0.9 copy.19
  161.4 0.0 copy-done
  161.4 0.9 copy.20
Async XLA Ops:
  156.5 4.1 %copy-start.1 = (f32[256,768]{1,0:T(8,128)S(1)}, f32[256,768]{1,0:T(8,128)}, u32[]{:S(2)}) copy-start(f32[256,768]{1,0:T(8,128)} %get-tuple-element.10) | copy-start | bytes 2359300
  156.5 5.0 %copy-start = (f32[256,768]{1,0:T(8,128)S(1)}, f32[256,768]{1,0:T(8,128)}, u32[]{:S(2)}) copy-start(f32[256,768]{1,0:T(8,128)} %get-tuple-element.11) | copy-start | bytes 2359300

commit v2 on v1

--- a/solution.py
+++ b/solution.py
@@ -32,11 +32,11 @@
 
 def kernel(
     ids_ref, p_ref, tgt_ref, inv_ref, x_ref, dy_ref, wg_hbm, wu_hbm, wd_hbm,
-    xg_ref, gg_ref, ug_ref, dg_ref,
+    xg_hbm, own_hbm, got_hbm,
     wgu, wd, pick, pickp, toa, tos,
     s_x, r_x, s_s, r_s, s_b, r_b, a_x, a_s, a_b,
-    act, gfac, hid, gu, xs, ss, dh, dgu, z_s, z_r,
-    wsem, lsem, sx_sem, rx_sem, sd_sem, rd_sem, sb_sem, rb_sem,
+    act, gfac, hid, gu, xs, ss, dh, dgu, z_s, own, xg,
+    wsem, osem, sx_sem, rx_sem, sd_sem, rd_sem, sb_sem, rb_sem,
     yx_s, yx_r, ys_s, ys_r, yh_s, yh_r, yg_s, yg_r, zz_s, zz_r,
 ):
     dpi = lax.axis_index("dp")
@@ -201,16 +201,32 @@
             gfac[part, cols] = up_pre * sig * (1.0 + gate_pre * (1.0 - sig))
             hid[part, cols] = (gate_act * up_pre).astype(BF16)
 
-    def hid_copy(k):
-        return to_y(hid, dh.at[k], yh_s.at[k], yh_r.at[k], k)
-
-    def gu_copy(k, h):
-        part = pl.ds(h * HALF, HALF)
-        return to_y(gu.at[part], dgu.at[k, part], yg_s.at[2 * k + h], yg_r.at[2 * k + h], k)
-
-    for k in range(1, NY):
-        hid_copy(k).start()
-        sent.append(hid_copy(k))
+    def piece_copy(src, dst, send, recv, size, k, q):
+        part = pl.ds(q * size, size)
+        n = k * (SLOTS // size) + q
+        if k == 2:
+            hop = 1 + 2 * (q % 2)
+            return to_y(dst.at[hop, part], dst.at[2, part], send.at[n], recv.at[n], hop)
+        return to_y(src.at[part], dst.at[k, part], send.at[n], recv.at[n], k)
+
+    def hid_copy(k, q):
+        return piece_copy(hid, dh, yh_s, yh_r, HALF, k, q)
+
+    def gu_copy(k, q):
+        return piece_copy(gu, dgu, yg_s, yg_r, ROWS, k, q)
+
+    def begin(copy):
+        copy.start()
+        sent.append(copy)
+
+    def pass_on(piece, even):
+        for q, hop in ((even, 1), (even + 1, 3)):
+            piece(hop, q).wait_recv()
+            begin(piece(2, q))
+
+    for q in range(2):
+        begin(hid_copy(1, q))
+        begin(hid_copy(3, 1 - q))
 
     for h in range(2):
         part = slice(h * HALF, (h + 1) * HALF)
@@ -224,9 +240,9 @@
             hidden_grad = dot(rows, wd[:, n * CW : (n + 1) * CW])
             gu[part, cols] = (hidden_grad * gfac[part, cols]).astype(BF16)
             gu[part, HW + n * CW : HW + (n + 1) * CW] = (hidden_grad * act[part, cols]).astype(BF16)
-        for k in range(1, NY):
-            gu_copy(k, h).start()
-            sent.append(gu_copy(k, h))
+        for q in range(2):
+            begin(gu_copy(1, 2 * h + q))
+            begin(gu_copy(3, 2 * h + 1 - q))
         deltas = gu[part, :]
         back = [
             dot(deltas, wgu[c * CW : (c + 1) * CW, :], 1, 1).astype(BF16) for c in range(CB)
@@ -237,67 +253,103 @@
                 [block[g * ROWS : (g + 1) * ROWS, :] for block in back]
             )
             start_group(s_b, r_b, sb_sem, rb_sem, j, -1)
+        if h == 0:
+            pass_on(hid_copy, 0)
+        else:
+            pass_on(gu_copy, 0)
 
     def z_copy(n):
         return pltpu.make_async_remote_copy(
             src_ref=z_s.at[n],
-            dst_ref=z_r.at[n],
+            dst_ref=got_hbm.at[n],
             send_sem=zz_s.at[n],
             recv_sem=zz_r.at[n],
             device_id=(partner, me),
             device_id_type=MESH,
         )
 
-    def sums(slices, own, b, right):
-        total = dot(own[b * NY + y], right(0), 0, 0)
+    def sums(slices, mine, b, right):
+        total = dot(mine[b * NY + y], right(0), 0, 0)
         for k in range(1, NY):
             total = total + dot(slices[k, b], right(k), 0, 0)
         return total
 
-    outs = (gg_ref, ug_ref, dg_ref)
-    wait_slices(a_s, ss, ys_s, ys_r)
-    for k in range(1, NY):
-        hid_copy(k).wait_recv()
-
     def hid_of(k):
         return hid[...] if k == 0 else dh[k]
 
-    z_s[2] = sums(ss, a_s, 1 - zl, hid_of).astype(BF16)
-    z_copy(2).start()
-    sent.append(z_copy(2))
-    dg_ref[...] = sums(ss, a_s, zl, hid_of)
+    def gate_of(k):
+        return gu[:, :HW] if k == 0 else dgu[k, :, :HW]
+
+    def up_of(k):
+        return gu[:, HW:] if k == 0 else dgu[k, :, HW:]
+
+    def send_sums(n, slices, mine, right):
+        z_s[n] = sums(slices, mine, 1 - zl, right).astype(BF16)
+        begin(z_copy(n))
+
+    def out_copy(n):
+        return pltpu.make_async_copy(own.at[n], own_hbm.at[n], osem.at[n])
+
+    def keep_sums(n, slices, mine, right):
+        own[n] = sums(slices, mine, zl, right)
+        out_copy(n).start()
+
+    wait_slices(a_s, ss, ys_s, ys_r)
+    for k, q in ((1, 1), (3, 0), (2, 0), (2, 1)):
+        hid_copy(k, q).wait_recv()
+    send_sums(2, ss, a_s, hid_of)
+    pass_on(gu_copy, 2)
+    keep_sums(2, ss, a_s, hid_of)
 
     wait_slices(a_x, xs, yx_s, yx_r)
-    for h in range(2):
-        for k in range(1, NY):
-            gu_copy(k, h).wait_recv()
-    for n in range(2):
-
-        def gu_of(k):
-            cols = slice(n * HW, (n + 1) * HW)
-            return gu[:, cols] if k == 0 else dgu[k, :, cols]
-
-        z_s[n] = sums(xs, a_x, 1 - zl, gu_of).astype(BF16)
-        z_copy(n).start()
-        sent.append(z_copy(n))
-    for n in range(2):
-
-        def gu_of(k):
-            cols = slice(n * HW, (n + 1) * HW)
-            return gu[:, cols] if k == 0 else dgu[k, :, cols]
-
-        outs[n][...] = sums(xs, a_x, zl, gu_of)
+    for k, q in ((1, 1), (3, 0), (1, 3), (3, 2), (2, 0), (2, 1), (2, 2), (2, 3)):
+        gu_copy(k, q).wait_recv()
+    send_sums(0, xs, a_x, gate_of)
+    send_sums(1, xs, a_x, up_of)
+    keep_sums(0, xs, a_x, gate_of)
+    keep_sums(1, xs, a_x, up_of)
 
     for j in range(NX):
         wait_group(s_b, r_b, sb_sem, rb_sem, j, -1)
         unpack(r_b, a_b, j)
     for c in range(CB):
-        xg_ref[:, c * CW : (c + 1) * CW] = dot(pick[...], a_b[c], 0, 0).astype(BF16)
+        xg[:, c * CW : (c + 1) * CW] = dot(pick[...], a_b[c], 0, 0).astype(BF16)
+    x_copy = pltpu.make_async_copy(xg, xg_hbm, osem.at[3])
+    x_copy.start()
+    for n in (2, 0, 1):
+        out_copy(n).wait()
+    x_copy.wait()
+    for copy in sent:
+        copy.wait_send()
     for n in (2, 0, 1):
         z_copy(n).wait_recv()
-        outs[n][...] += z_r[n].astype(F32)
-    for copy in sent:
-        copy.wait_send()
+
+
+def finish(xg_in, own_in, got_in, xg_out, g_out, u_out, d_out, xv, own, got, isem, osem):
+    loads = [
+        (
+            pltpu.make_async_copy(own_in.at[n], own.at[n], isem.at[n]),
+            pltpu.make_async_copy(got_in.at[n], got.at[n], isem.at[3 + n]),
+        )
+        for n in range(3)
+    ]
+    x_load = pltpu.make_async_copy(xg_in, xv, isem.at[6])
+    for a, b in loads:
+        a.start()
+        b.start()
+    x_load.start()
+    stores = []
+    for n, out in enumerate((g_out, u_out, d_out)):
+        for load in loads[n]:
+            load.wait()
+        own[n] += got[n].astype(F32)
+        stores.append(pltpu.make_async_copy(own.at[n], out, osem.at[n]))
+        stores[-1].start()
+    x_load.wait()
+    stores.append(pltpu.make_async_copy(xv, xg_out, osem.at[3]))
+    stores[-1].start()
+    for store in stores:
+        store.wait()
 
 
 def on_device(x_tokens, dy_tokens, probs, ids, w_gate, w_up, w_down):
@@ -311,11 +363,17 @@
     grad = jax.ShapeDtypeStruct((D // 8, HW), F32)
     chunks = pltpu.VMEM((NX * GROUP, CW), BF16)
     slots = pltpu.VMEM((CB, SLOTS, CW), BF16)
-    x_grad, gate_grad, up_grad, down_grad = pl.pallas_call(
+    x_grad = jax.ShapeDtypeStruct((TOK, D), BF16)
+    thirds = (3, D // 8, HW)
+    parts = pl.pallas_call(
         kernel,
-        out_shape=(jax.ShapeDtypeStruct((TOK, D), BF16), grad, grad, grad),
+        out_shape=(
+            x_grad,
+            jax.ShapeDtypeStruct(thirds, F32),
+            jax.ShapeDtypeStruct(thirds, BF16),
+        ),
         in_specs=[vmem] * 6 + [anywhere] * 3,
-        out_specs=[vmem] * 4,
+        out_specs=[anywhere] * 3,
         scratch_shapes=[
             pltpu.VMEM((D, 2 * HW), BF16),
             pltpu.VMEM((D, HW), BF16),
@@ -335,15 +393,16 @@
             pltpu.VMEM((NY, 2, SLOTS, CW), BF16),
             pltpu.VMEM((NY, SLOTS, HW), BF16),
             pltpu.VMEM((NY, SLOTS, 2 * HW), BF16),
-            pltpu.VMEM((3, D // 8, HW), BF16),
-            pltpu.VMEM((3, D // 8, HW), BF16),
+            pltpu.VMEM(thirds, BF16),
+            pltpu.VMEM(thirds, F32),
+            pltpu.VMEM((TOK, D), BF16),
             dma((3,)),
-            dma((1,)),
+            dma((4,)),
         ]
         + [dma((NX * ZC,))] * 6
         + [dma((4 * NY,))] * 4
-        + [dma((NY,))] * 2
         + [dma((2 * NY,))] * 2
+        + [dma((4 * NY,))] * 2
         + [dma((3,))] * 2,
         compiler_params=pltpu.CompilerParams(
             collective_id=0, has_side_effects=True, vmem_limit_bytes=60 << 20
@@ -359,6 +418,19 @@
         w_up,
         w_down,
     )
+    x_grad, gate_grad, up_grad, down_grad = pl.pallas_call(
+        finish,
+        out_shape=(x_grad, grad, grad, grad),
+        in_specs=[anywhere] * 3,
+        out_specs=[anywhere] * 4,
+        scratch_shapes=[
+            pltpu.VMEM((TOK, D), BF16),
+            pltpu.VMEM(thirds, F32),
+            pltpu.VMEM(thirds, BF16),
+            dma((7,)),
+            dma((4,)),
+        ],
+    )(*parts)
     return (x_grad, gate_grad[None], up_grad[None], down_grad[None])
 
 

time: 163 us -> 143 us (0.88)
  Pallas kernels: 156 us -> 142 us
  local copies, waits for them, and re-layouts: 5.83 us -> 0 us
    pallas_call x1 -> x2, Pallas kernels: 156 us -> 142 us  [the longest x1 139 us: on_device(): pl.pallas_call(kernel, out_shape=(x_grad, jax.ShapeDtypeStruct(thirds, F3...]
    unnamed x8 -> x0, local copies, waits for them, and re-layouts: 5.83 us -> none
where the time goes in v2:
time: 143 us
  Pallas kernels  142 us (99%)
    pallas_call x1, Pallas kernels, on_device(): pl.pallas_call(kernel, out_shape=(x_grad, jax.ShapeDtypeStruct(thirds, F3...  139 us
    pallas_call x1, Pallas kernels, on_device(): pl.pallas_call(finish, out_shape=(x_grad, grad, grad, grad), in_specs=[an...  3.16 us

profile of v2, /device:TPU:1, one launch (start us, length us, event | category | flops | bytes accessed | tf_op | source)
XLA Modules:
  0.0 142.6 jit_solution(3361069011981451944)
XLA Ops:
  0.6 138.7 %shard_map.120 = (bf16[128,2048]{1,0:T(8,128)(2,1)}, f32[3,256,768]{2,1,0:T(8,128)}, bf16[3,256,768]{2,1,0:T(8,128)(2,1)}) custom-call(s32[8,128]{1,0:T(8,128)} %bitcast.5, bf16[8,128]{1,0:T(8,128)(2,1)} %bitcast.6, s32[1,640]{1,0:T(1,128)} %constant.10.tgt_ref.inv_ref, s32[1,640]{1,0:T(1,128)} %constant.10.tgt_ref.inv_ref, bf16[128,2048]{1,0:T(8,128)(2,1)} %x_ref.1, ...), custom_call_target="tpu_custom_call" | custom-call | tf_op jit(solution)/shard_map/pallas_call | solution.py:368
  139.3 3.2 %shard_map.121 = (bf16[128,2048]{1,0:T(8,128)(2,1)}, f32[256,768]{1,0:T(8,128)}, f32[256,768]{1,0:T(8,128)}, f32[256,768]{1,0:T(8,128)}) custom-call(bf16[128,2048]{1,0:T(8,128)(2,1)} %get-tuple-element.11.xg_in, f32[3,256,768]{2,1,0:T(8,128)} %get-tuple-element.12.own_in, bf16[3,256,768]{2,1,0:T(8,128)(2,1)} %get-tuple-element.13.got_in), custom_call_target="tpu_custom_call" | custom-call | tf_op jit(solution)/shard_map/pallas_call | solution.py:421

commit v3 on v2

--- a/solution.py
+++ b/solution.py
@@ -23,7 +23,7 @@
 CHUNK = CB * CAP
 GROUP = ZC * CHUNK
 SLOTS = NX * ROWS
-HALF = 2 * ROWS
+AHEAD = 3
 
 
 def dot(a, b, ca=1, cb=0):
@@ -140,14 +140,21 @@
             [rows[:, c * CW : (c + 1) * CW] for c in range(CB)]
         )
 
-    for j in range(NX):
-        gather(pick, x_ref, s_x, j)
-        if j == 0:
+    def start_out(n):
+        if n % 2 == 0 and n < 2 * NX:
+            start_group(s_x, r_x, sx_sem, rx_sem, n // 2, 1)
+        elif n < 2 * NX:
+            start_group(s_s, r_s, sd_sem, rd_sem, n // 2, 1)
+
+    for n in range(2 * NX):
+        if n % 2 == 0:
+            gather(pick, x_ref, s_x, n // 2)
+        else:
+            gather(pickp, dy_ref, s_s, n // 2)
+        if n == 0:
             pl.semaphore_wait(barrier, NX * ZC - 1 + NY)
-        start_group(s_x, r_x, sx_sem, rx_sem, j, 1)
-    for j in range(NX):
-        gather(pickp, dy_ref, s_s, j)
-        start_group(s_s, r_s, sd_sem, rd_sem, j, 1)
+        if n < AHEAD:
+            start_out(n)
 
     def to_y(src, dst, send, recv, k):
         return pltpu.make_async_remote_copy(
@@ -159,37 +166,65 @@
             device_id_type=MESH,
         )
 
-    def slice_copy(src, dst, send, recv, k, b, h):
-        part = pl.ds(h * HALF, HALF)
-        n = (k * 2 + b) * 2 + h
+    def slice_copy(src, dst, send, recv, k, b, j):
+        part = pl.ds(j * ROWS, ROWS)
+        n = ((k - 1) * 2 + b) * NX + j
         yt = lax.rem(y + k, NY)
         return to_y(
             src.at[b * NY + yt, part], dst.at[k, b, part], send.at[n], recv.at[n], k
         )
 
-    def start_slices(src, dst, send, recv, h):
+    def start_slices(src, dst, send, recv, j):
         for k in range(1, NY):
             for b in range(2):
-                copy = slice_copy(src, dst, send, recv, k, b, h)
+                copy = slice_copy(src, dst, send, recv, k, b, j)
                 copy.start()
                 sent.append(copy)
 
     def wait_slices(src, dst, send, recv):
-        for h in range(2):
+        for j in range(NX):
             for k in range(1, NY):
                 for b in range(2):
-                    slice_copy(src, dst, send, recv, k, b, h).wait_recv()
-
-    for h in range(2):
-        for j in (2 * h, 2 * h + 1):
-            wait_group(s_x, r_x, sx_sem, rx_sem, j, 1)
-            unpack(r_x, a_x, j)
-        start_slices(a_x, xs, yx_s, yx_r, h)
-
-    for load in loads:
-        load.wait()
-    for h in range(2):
-        part = slice(h * HALF, (h + 1) * HALF)
+                    slice_copy(src, dst, send, recv, k, b, j).wait_recv()
+
+    def piece_copy(src, dst, send, recv, k, q):
+        part = pl.ds(q * ROWS, ROWS)
+        n = (k - 1) * NX + q
+        if k == 2:
+            hop = 1 + 2 * (q % 2)
+            return to_y(dst.at[hop, part], dst.at[2, part], send.at[n], recv.at[n], hop)
+        return to_y(src.at[part], dst.at[k, part], send.at[n], recv.at[n], k)
+
+    def hid_copy(k, q):
+        return piece_copy(hid, dh, yh_s, yh_r, k, q)
+
+    def gu_copy(k, q):
+        return piece_copy(gu, dgu, yg_s, yg_r, k, q)
+
+    def begin(copy):
+        copy.start()
+        sent.append(copy)
+
+    def pass_on(piece, q):
+        piece(1 + 2 * (q % 2), q).wait_recv()
+        begin(piece(2, q))
+
+    def start_piece(piece, q):
+        begin(piece(1 + 2 * (q % 2), q))
+        begin(piece(3 - 2 * (q % 2), q))
+
+    def start_back(j):
+        start_group(s_b, r_b, sb_sem, rb_sem, j, -1)
+
+    for j in range(NX):
+        part = slice(j * ROWS, (j + 1) * ROWS)
+        wait_group(s_x, r_x, sx_sem, rx_sem, j, 1)
+        start_out(2 * j + AHEAD)
+        unpack(r_x, a_x, j)
+        start_slices(a_x, xs, yx_s, yx_r, j)
+        if j == 0:
+            for load in loads:
+                load.wait()
         rows = jnp.concatenate([a_x[c, part, :] for c in range(CB)], axis=1)
         for n in range(HW // CW):
             cols = slice(n * CW, (n + 1) * CW)
@@ -200,63 +235,39 @@
             act[part, cols] = gate_act
             gfac[part, cols] = up_pre * sig * (1.0 + gate_pre * (1.0 - sig))
             hid[part, cols] = (gate_act * up_pre).astype(BF16)
-
-    def piece_copy(src, dst, send, recv, size, k, q):
-        part = pl.ds(q * size, size)
-        n = k * (SLOTS // size) + q
-        if k == 2:
-            hop = 1 + 2 * (q % 2)
-            return to_y(dst.at[hop, part], dst.at[2, part], send.at[n], recv.at[n], hop)
-        return to_y(src.at[part], dst.at[k, part], send.at[n], recv.at[n], k)
-
-    def hid_copy(k, q):
-        return piece_copy(hid, dh, yh_s, yh_r, HALF, k, q)
-
-    def gu_copy(k, q):
-        return piece_copy(gu, dgu, yg_s, yg_r, ROWS, k, q)
-
-    def begin(copy):
-        copy.start()
-        sent.append(copy)
-
-    def pass_on(piece, even):
-        for q, hop in ((even, 1), (even + 1, 3)):
-            piece(hop, q).wait_recv()
-            begin(piece(2, q))
-
-    for q in range(2):
-        begin(hid_copy(1, q))
-        begin(hid_copy(3, 1 - q))
-
-    for h in range(2):
-        part = slice(h * HALF, (h + 1) * HALF)
-        for j in (2 * h, 2 * h + 1):
-            wait_group(s_s, r_s, sd_sem, rd_sem, j, 1)
-            unpack(r_s, a_s, j)
-        start_slices(a_s, ss, ys_s, ys_r, h)
+        if j == NX - 1:
+            start_back(0)
+        else:
+            start_piece(hid_copy, j)
+        wait_group(s_s, r_s, sd_sem, rd_sem, j, 1)
+        start_out(2 * j + 1 + AHEAD)
+        if j == NX - 1:
+            start_back(1)
+            start_back(2)
+        unpack(r_s, a_s, j)
         rows = jnp.concatenate([a_s[c, part, :] for c in range(CB)], axis=1)
         for n in range(HW // CW):
             cols = slice(n * CW, (n + 1) * CW)
             hidden_grad = dot(rows, wd[:, n * CW : (n + 1) * CW])
             gu[part, cols] = (hidden_grad * gfac[part, cols]).astype(BF16)
             gu[part, HW + n * CW : HW + (n + 1) * CW] = (hidden_grad * act[part, cols]).astype(BF16)
-        for q in range(2):
-            begin(gu_copy(1, 2 * h + q))
-            begin(gu_copy(3, 2 * h + 1 - q))
+        start_piece(gu_copy, j)
         deltas = gu[part, :]
-        back = [
-            dot(deltas, wgu[c * CW : (c + 1) * CW, :], 1, 1).astype(BF16) for c in range(CB)
-        ]
-        for g in range(2):
-            j = 2 * h + g
-            s_b[j * GROUP : (j + 1) * GROUP, :] = pack(
-                [block[g * ROWS : (g + 1) * ROWS, :] for block in back]
-            )
-            start_group(s_b, r_b, sb_sem, rb_sem, j, -1)
-        if h == 0:
-            pass_on(hid_copy, 0)
-        else:
-            pass_on(gu_copy, 0)
+        s_b[j * GROUP : (j + 1) * GROUP, :] = pack(
+            [dot(deltas, wgu[c * CW : (c + 1) * CW, :], 1, 1).astype(BF16) for c in range(CB)]
+        )
+        if j == NX - 1:
+            start_back(j)
+        if j > 0:
+            pass_on(gu_copy, j - 1)
+            if j < NX - 1:
+                pass_on(hid_copy, j - 1)
+    start_piece(hid_copy, NX - 1)
+    pass_on(gu_copy, NX - 1)
+    for j in range(NX):
+        start_slices(a_s, ss, ys_s, ys_r, j)
+        if j > 1:
+            pass_on(hid_copy, j)
 
     def z_copy(n):
         return pltpu.make_async_remote_copy(
@@ -294,20 +305,21 @@
         own[n] = sums(slices, mine, zl, right)
         out_copy(n).start()
 
-    wait_slices(a_s, ss, ys_s, ys_r)
-    for k, q in ((1, 1), (3, 0), (2, 0), (2, 1)):
-        hid_copy(k, q).wait_recv()
-    send_sums(2, ss, a_s, hid_of)
-    pass_on(gu_copy, 2)
-    keep_sums(2, ss, a_s, hid_of)
+    def wait_pieces(piece):
+        for q in range(NX):
+            piece(3 - 2 * (q % 2), q).wait_recv()
+            piece(2, q).wait_recv()
 
     wait_slices(a_x, xs, yx_s, yx_r)
-    for k, q in ((1, 1), (3, 0), (1, 3), (3, 2), (2, 0), (2, 1), (2, 2), (2, 3)):
-        gu_copy(k, q).wait_recv()
+    wait_pieces(gu_copy)
     send_sums(0, xs, a_x, gate_of)
     send_sums(1, xs, a_x, up_of)
+    wait_slices(a_s, ss, ys_s, ys_r)
+    wait_pieces(hid_copy)
+    send_sums(2, ss, a_s, hid_of)
     keep_sums(0, xs, a_x, gate_of)
     keep_sums(1, xs, a_x, up_of)
+    keep_sums(2, ss, a_s, hid_of)
 
     for j in range(NX):
         wait_group(s_b, r_b, sb_sem, rb_sem, j, -1)
@@ -400,9 +412,8 @@
             dma((4,)),
         ]
         + [dma((NX * ZC,))] * 6
-        + [dma((4 * NY,))] * 4
-        + [dma((2 * NY,))] * 2
-        + [dma((4 * NY,))] * 2
+        + [dma((6 * NX,))] * 4
+        + [dma((3 * NX,))] * 4
         + [dma((3,))] * 2,
         compiler_params=pltpu.CompilerParams(
             collective_id=0, has_side_effects=True, vmem_limit_bytes=60 << 20

time: 143 us -> 131 us (0.916)
  Pallas kernels: 142 us -> 130 us
    pallas_call x1, Pallas kernels: 139 us -> 127 us  [on_device(): pl.pallas_call(kernel, out_shape=(x_grad, jax.ShapeDtypeStruct(thirds, F3...]
where the time goes in v3:
time: 131 us
  Pallas kernels  130 us (99%)
    pallas_call x1, Pallas kernels, on_device(): pl.pallas_call(kernel, out_shape=(x_grad, jax.ShapeDtypeStruct(thirds, F3...  127 us
    pallas_call x1, Pallas kernels, on_device(): pl.pallas_call(finish, out_shape=(x_grad, grad, grad, grad), in_specs=[an...  3.16 us

profile of v3, /device:TPU:1, one launch (start us, length us, event | category | flops | bytes accessed | tf_op | source)
XLA Modules:
  0.0 131.3 jit_solution(12499605647313591339)
XLA Ops:
  0.6 127.3 %shard_map.120 = (bf16[128,2048]{1,0:T(8,128)(2,1)}, f32[3,256,768]{2,1,0:T(8,128)}, bf16[3,256,768]{2,1,0:T(8,128)(2,1)}) custom-call(s32[8,128]{1,0:T(8,128)} %bitcast.5, bf16[8,128]{1,0:T(8,128)(2,1)} %bitcast.6, s32[1,640]{1,0:T(1,128)} %constant.10.tgt_ref.inv_ref, s32[1,640]{1,0:T(1,128)} %constant.10.tgt_ref.inv_ref, bf16[128,2048]{1,0:T(8,128)(2,1)} %x_ref.1, ...), custom_call_target="tpu_custom_call" | custom-call | tf_op jit(solution)/shard_map/pallas_call | solution.py:380
  127.9 3.2 %shard_map.121 = (bf16[128,2048]{1,0:T(8,128)(2,1)}, f32[256,768]{1,0:T(8,128)}, f32[256,768]{1,0:T(8,128)}, f32[256,768]{1,0:T(8,128)}) custom-call(bf16[128,2048]{1,0:T(8,128)(2,1)} %get-tuple-element.11.xg_in, f32[3,256,768]{2,1,0:T(8,128)} %get-tuple-element.12.own_in, bf16[3,256,768]{2,1,0:T(8,128)(2,1)} %get-tuple-element.13.got_in), custom_call_target="tpu_custom_call" | custom-call | tf_op jit(solution)/shard_map/pallas_call | solution.py:432

commit v4 on v3

--- a/solution.py
+++ b/solution.py
@@ -15,7 +15,8 @@
 D = 2048
 HW = 768
 NX = 4
-ZC = 8
+NZ = 4
+ZC = 2 * NZ
 NY = 4
 CB = 8
 CW = D // CB
@@ -43,6 +44,7 @@
     me = lax.axis_index("expert")
     zl, y = dpi // NY, lax.rem(dpi, NY)
     xi, zc = me // ZC, lax.rem(me, ZC)
+    zh, core = zc // 2, lax.rem(zc, 2)
 
     loads = [
         pltpu.make_async_copy(wg_hbm.at[0], wgu.at[:, pl.ds(0, HW)], wsem.at[0]),
@@ -53,10 +55,18 @@
         load.start()
 
     barrier = pltpu.get_barrier_semaphore()
-    for k in range(1, NX * ZC):
-        pl.semaphore_signal(
-            barrier, inc=1, device_id=(dpi, lax.rem(me + k, NX * ZC)), device_id_type=MESH
-        )
+    met = ((zl, 0), (zl, 1), (zl, 3), (1 - zl, 2), (1 - zl, 3 - 2 * zl))
+    for n, (zlt, far) in enumerate(met):
+        for k in range(2 * NX):
+            if n or k:
+                other = (
+                    lax.rem(xi + k // 2, NX) * ZC
+                    + lax.rem(zh + far, NZ) * 2
+                    + lax.rem(core + k, 2)
+                )
+                pl.semaphore_signal(
+                    barrier, inc=1, device_id=(zlt * NY + y, other), device_id_type=MESH
+                )
     for k in range(1, NY):
         pl.semaphore_signal(
             barrier, inc=1, device_id=(zl * NY + lax.rem(y + k, NY), me), device_id_type=MESH
@@ -94,18 +104,42 @@
     toa[...] = jnp.where(down == inv_ref[...], 1.0, 0.0).astype(BF16)
 
     def exchange(src, dst, send, recv, j, i, sign):
-        zt = lax.rem(zc + i, ZC)
+        far, flip = i // 2, i % 2
+        ct = lax.rem(core + flip, 2)
         xt = lax.rem(xi + sign * j + NX, NX)
-        from_rows = pl.ds(pl.multiple_of((j * ZC + zt) * CHUNK, 16), CHUNK)
-        to_rows = pl.ds(pl.multiple_of((j * ZC + zc) * CHUNK, 16), CHUNK)
+        if sign > 0:
+            zt = lax.rem(zh + far, NZ)
+            zlt = (zl, 0, 1 - zl, 1)[far]
+            take = zt * 2 + ct
+            spot = (0, 1 + 2 * zl, 2, 1 + 2 * zl)[far]
+            put = spot * 2 + core
+        else:
+            zt = lax.rem(zh + (0, 3 - 2 * zl, 2, 3 - 2 * zl)[far], NZ)
+            zlt = (zl, 0, 1 - zl, 1)[far]
+            take = far * 2 + ct
+            spot = (0, 1 + 2 * zl, 2, 1 + 2 * zl)[far]
+            put = zc
+        from_rows = pl.ds(pl.multiple_of((j * ZC + take) * CHUNK, 16), CHUNK)
+        to_rows = pl.ds(pl.multiple_of((j * ZC + put) * CHUNK, 16), CHUNK)
         if i == 0 and j == 0:
             return pltpu.make_async_copy(src.at[from_rows], dst.at[to_rows], recv.at[0])
         return pltpu.make_async_remote_copy(
             src_ref=src.at[from_rows],
             dst_ref=dst.at[to_rows],
             send_sem=send.at[j * ZC + i],
+            recv_sem=recv.at[j * ZC + spot * 2 + flip],
+            device_id=(zlt * NY + y, xt * ZC + zt * 2 + ct),
+            device_id_type=MESH,
+        )
+
+    def arrival(src, dst, send, recv, j, i):
+        rows = pl.ds((j * ZC + i) * CHUNK, CHUNK)
+        return pltpu.make_async_remote_copy(
+            src_ref=src.at[rows],
+            dst_ref=dst.at[rows],
+            send_sem=send.at[j * ZC + i],
             recv_sem=recv.at[j * ZC + i],
-            device_id=(dpi, xt * ZC + zt),
+            device_id=(partner, me),
             device_id_type=MESH,
         )
 
@@ -120,11 +154,10 @@
 
     def wait_group(src, dst, send, recv, j, sign):
         for i in range(ZC):
-            copy = exchange(src, dst, send, recv, j, i, sign)
             if i or j:
-                copy.wait_recv()
+                arrival(src, dst, send, recv, j, i).wait_recv()
             else:
-                copy.wait()
+                exchange(src, dst, send, recv, j, i, sign).wait()
 
     def pack(blocks):
         return dot(tos[...], jnp.concatenate(blocks, axis=0)).astype(BF16)
@@ -152,7 +185,7 @@
         else:
             gather(pickp, dy_ref, s_s, n // 2)
         if n == 0:
-            pl.semaphore_wait(barrier, NX * ZC - 1 + NY)
+            pl.semaphore_wait(barrier, 10 * NX - 1 + NY)
         if n < AHEAD:
             start_out(n)
 
@@ -166,26 +199,27 @@
             device_id_type=MESH,
         )
 
+    def block_of(b):
+        return zl if b else 1 - zl
+
     def slice_copy(src, dst, send, recv, k, b, j):
         part = pl.ds(j * ROWS, ROWS)
         n = ((k - 1) * 2 + b) * NX + j
         yt = lax.rem(y + k, NY)
         return to_y(
-            src.at[b * NY + yt, part], dst.at[k, b, part], send.at[n], recv.at[n], k
-        )
-
-    def start_slices(src, dst, send, recv, j):
+            src.at[block_of(b) * NY + yt, part], dst.at[k, b, part], send.at[n], recv.at[n], k
+        )
+
+    def start_slices(src, dst, send, recv, j, b):
         for k in range(1, NY):
-            for b in range(2):
-                copy = slice_copy(src, dst, send, recv, k, b, j)
-                copy.start()
-                sent.append(copy)
-
-    def wait_slices(src, dst, send, recv):
+            copy = slice_copy(src, dst, send, recv, k, b, j)
+            copy.start()
+            sent.append(copy)
+
+    def wait_slices(src, dst, send, recv, b):
         for j in range(NX):
             for k in range(1, NY):
-                for b in range(2):
-                    slice_copy(src, dst, send, recv, k, b, j).wait_recv()
+                slice_copy(src, dst, send, recv, k, b, j).wait_recv()
 
     def piece_copy(src, dst, send, recv, k, q):
         part = pl.ds(q * ROWS, ROWS)
@@ -221,7 +255,7 @@
         wait_group(s_x, r_x, sx_sem, rx_sem, j, 1)
         start_out(2 * j + AHEAD)
         unpack(r_x, a_x, j)
-        start_slices(a_x, xs, yx_s, yx_r, j)
+        start_slices(a_x, xs, yx_s, yx_r, j, 0)
         if j == 0:
             for load in loads:
                 load.wait()
@@ -235,10 +269,9 @@
             act[part, cols] = gate_act
             gfac[part, cols] = up_pre * sig * (1.0 + gate_pre * (1.0 - sig))
             hid[part, cols] = (gate_act * up_pre).astype(BF16)
+        start_piece(hid_copy, j)
         if j == NX - 1:
             start_back(0)
-        else:
-            start_piece(hid_copy, j)
         wait_group(s_s, r_s, sd_sem, rd_sem, j, 1)
         start_out(2 * j + 1 + AHEAD)
         if j == NX - 1:
@@ -251,6 +284,7 @@
             hidden_grad = dot(rows, wd[:, n * CW : (n + 1) * CW])
             gu[part, cols] = (hidden_grad * gfac[part, cols]).astype(BF16)
             gu[part, HW + n * CW : HW + (n + 1) * CW] = (hidden_grad * act[part, cols]).astype(BF16)
+        start_slices(a_s, ss, ys_s, ys_r, j, 0)
         start_piece(gu_copy, j)
         deltas = gu[part, :]
         s_b[j * GROUP : (j + 1) * GROUP, :] = pack(
@@ -260,14 +294,8 @@
             start_back(j)
         if j > 0:
             pass_on(gu_copy, j - 1)
-            if j < NX - 1:
-                pass_on(hid_copy, j - 1)
-    start_piece(hid_copy, NX - 1)
-    pass_on(gu_copy, NX - 1)
-    for j in range(NX):
-        start_slices(a_s, ss, ys_s, ys_r, j)
-        if j > 1:
-            pass_on(hid_copy, j)
+            pass_on(hid_copy, j - 1)
+    pass_on(hid_copy, NX - 1)
 
     def z_copy(n):
         return pltpu.make_async_remote_copy(
@@ -280,7 +308,7 @@
         )
 
     def sums(slices, mine, b, right):
-        total = dot(mine[b * NY + y], right(0), 0, 0)
+        total = dot(mine[block_of(b) * NY + y], right(0), 0, 0)
         for k in range(1, NY):
             total = total + dot(slices[k, b], right(k), 0, 0)
         return total
@@ -295,14 +323,14 @@
         return gu[:, HW:] if k == 0 else dgu[k, :, HW:]
 
     def send_sums(n, slices, mine, right):
-        z_s[n] = sums(slices, mine, 1 - zl, right).astype(BF16)
+        z_s[n] = sums(slices, mine, 0, right).astype(BF16)
         begin(z_copy(n))
 
     def out_copy(n):
         return pltpu.make_async_copy(own.at[n], own_hbm.at[n], osem.at[n])
 
     def keep_sums(n, slices, mine, right):
-        own[n] = sums(slices, mine, zl, right)
+        own[n] = sums(slices, mine, 1, right)
         out_copy(n).start()
 
     def wait_pieces(piece):
@@ -310,22 +338,28 @@
             piece(3 - 2 * (q % 2), q).wait_recv()
             piece(2, q).wait_recv()
 
-    wait_slices(a_x, xs, yx_s, yx_r)
+    pass_on(gu_copy, NX - 1)
+    for j in range(NX):
+        start_slices(a_s, ss, ys_s, ys_r, j, 1)
+        start_slices(a_x, xs, yx_s, yx_r, j, 1)
+    wait_slices(a_s, ss, ys_s, ys_r, 0)
+    wait_pieces(hid_copy)
+    send_sums(2, ss, a_s, hid_of)
+    wait_slices(a_x, xs, yx_s, yx_r, 0)
     wait_pieces(gu_copy)
     send_sums(0, xs, a_x, gate_of)
     send_sums(1, xs, a_x, up_of)
-    wait_slices(a_s, ss, ys_s, ys_r)
-    wait_pieces(hid_copy)
-    send_sums(2, ss, a_s, hid_of)
-    keep_sums(0, xs, a_x, gate_of)
-    keep_sums(1, xs, a_x, up_of)
-    keep_sums(2, ss, a_s, hid_of)
 
     for j in range(NX):
         wait_group(s_b, r_b, sb_sem, rb_sem, j, -1)
         unpack(r_b, a_b, j)
     for c in range(CB):
         xg[:, c * CW : (c + 1) * CW] = dot(pick[...], a_b[c], 0, 0).astype(BF16)
+    wait_slices(a_s, ss, ys_s, ys_r, 1)
+    keep_sums(2, ss, a_s, hid_of)
+    wait_slices(a_x, xs, yx_s, yx_r, 1)
+    keep_sums(0, xs, a_x, gate_of)
+    keep_sums(1, xs, a_x, up_of)
     x_copy = pltpu.make_async_copy(xg, xg_hbm, osem.at[3])
     x_copy.start()
     for n in (2, 0, 1):

time: 131 us -> 135 us (1.031)
  Pallas kernels: 130 us -> 134 us
    pallas_call x1, Pallas kernels: 127 us -> 131 us  [on_device(): pl.pallas_call(kernel, out_shape=(x_grad, jax.ShapeDtypeStruct(thirds, F3...]
where the time goes in v4:
time: 135 us
  Pallas kernels  134 us (99%)
    pallas_call x1, Pallas kernels, on_device(): pl.pallas_call(kernel, out_shape=(x_grad, jax.ShapeDtypeStruct(thirds, F3...  131 us
    pallas_call x1, Pallas kernels, on_device(): pl.pallas_call(finish, out_shape=(x_grad, grad, grad, grad), in_specs=[an...  3.16 us

profile of v4, /device:TPU:1, one launch (start us, length us, event | category | flops | bytes accessed | tf_op | source)
XLA Modules:
  0.0 134.7 jit_solution(7437264303674426833)
XLA Ops:
  0.6 130.8 %shard_map.120 = (bf16[128,2048]{1,0:T(8,128)(2,1)}, f32[3,256,768]{2,1,0:T(8,128)}, bf16[3,256,768]{2,1,0:T(8,128)(2,1)}) custom-call(s32[8,128]{1,0:T(8,128)} %bitcast.5, bf16[8,128]{1,0:T(8,128)(2,1)} %bitcast.6, s32[1,640]{1,0:T(1,128)} %constant.10.tgt_ref.inv_ref, s32[1,640]{1,0:T(1,128)} %constant.10.tgt_ref.inv_ref, bf16[128,2048]{1,0:T(8,128)(2,1)} %x_ref.1, ...), custom_call_target="tpu_custom_call" | custom-call | tf_op jit(solution)/shard_map/pallas_call | solution.py:414
  131.4 3.2 %shard_map.121 = (bf16[128,2048]{1,0:T(8,128)(2,1)}, f32[256,768]{1,0:T(8,128)}, f32[256,768]{1,0:T(8,128)}, f32[256,768]{1,0:T(8,128)}) custom-call(bf16[128,2048]{1,0:T(8,128)(2,1)} %get-tuple-element.11.xg_in, f32[3,256,768]{2,1,0:T(8,128)} %get-tuple-element.12.own_in, bf16[3,256,768]{2,1,0:T(8,128)(2,1)} %get-tuple-element.13.got_in), custom_call_target="tpu_custom_call" | custom-call | tf_op jit(solution)/shard_map/pallas_call | solution.py:466

commit v5 on v4

--- a/solution.py
+++ b/solution.py
@@ -38,7 +38,7 @@
     s_x, r_x, s_s, r_s, s_b, r_b, a_x, a_s, a_b,
     act, gfac, hid, gu, xs, ss, dh, dgu, z_s, own, xg,
     wsem, osem, sx_sem, rx_sem, sd_sem, rd_sem, sb_sem, rb_sem,
-    yx_s, yx_r, ys_s, ys_r, yh_s, yh_r, yg_s, yg_r, zz_s, zz_r,
+    yx_s, yx_r, ys_s, ys_r, yh_s, yh_r, yg_s, yg_r, yu_s, yu_r, zz_s, zz_r,
 ):
     dpi = lax.axis_index("dp")
     me = lax.axis_index("expert")
@@ -232,8 +232,13 @@
     def hid_copy(k, q):
         return piece_copy(hid, dh, yh_s, yh_r, k, q)
 
-    def gu_copy(k, q):
-        return piece_copy(gu, dgu, yg_s, yg_r, k, q)
+    def gate_copy(k, q):
+        cols = pl.ds(0, HW)
+        return piece_copy(gu.at[:, cols], dgu.at[:, :, cols], yg_s, yg_r, k, q)
+
+    def up_copy(k, q):
+        cols = pl.ds(HW, HW)
+        return piece_copy(gu.at[:, cols], dgu.at[:, :, cols], yu_s, yu_r, k, q)
 
     def begin(copy):
         copy.start()
@@ -285,7 +290,7 @@
             gu[part, cols] = (hidden_grad * gfac[part, cols]).astype(BF16)
             gu[part, HW + n * CW : HW + (n + 1) * CW] = (hidden_grad * act[part, cols]).astype(BF16)
         start_slices(a_s, ss, ys_s, ys_r, j, 0)
-        start_piece(gu_copy, j)
+        start_piece(gate_copy, j)
         deltas = gu[part, :]
         s_b[j * GROUP : (j + 1) * GROUP, :] = pack(
             [dot(deltas, wgu[c * CW : (c + 1) * CW, :], 1, 1).astype(BF16) for c in range(CB)]
@@ -293,8 +298,10 @@
         if j == NX - 1:
             start_back(j)
         if j > 0:
-            pass_on(gu_copy, j - 1)
             pass_on(hid_copy, j - 1)
+            pass_on(gate_copy, j - 1)
+            if j < NX - 1:
+                start_piece(up_copy, j - 1)
     pass_on(hid_copy, NX - 1)
 
     def z_copy(n):
@@ -338,16 +345,25 @@
             piece(3 - 2 * (q % 2), q).wait_recv()
             piece(2, q).wait_recv()
 
-    pass_on(gu_copy, NX - 1)
+    pass_on(gate_copy, NX - 1)
     for j in range(NX):
-        start_slices(a_s, ss, ys_s, ys_r, j, 1)
-        start_slices(a_x, xs, yx_s, yx_r, j, 1)
+        if j < 2:
+            start_piece(up_copy, NX - 2 + j)
+        else:
+            pass_on(up_copy, j - 2)
     wait_slices(a_s, ss, ys_s, ys_r, 0)
     wait_pieces(hid_copy)
     send_sums(2, ss, a_s, hid_of)
     wait_slices(a_x, xs, yx_s, yx_r, 0)
-    wait_pieces(gu_copy)
+    wait_pieces(gate_copy)
     send_sums(0, xs, a_x, gate_of)
+    for j in range(NX):
+        if j > 1:
+            pass_on(up_copy, j)
+    for j in range(NX):
+        start_slices(a_s, ss, ys_s, ys_r, j, 1)
+        start_slices(a_x, xs, yx_s, yx_r, j, 1)
+    wait_pieces(up_copy)
     send_sums(1, xs, a_x, up_of)
 
     for j in range(NX):
@@ -447,7 +463,7 @@
         ]
         + [dma((NX * ZC,))] * 6
         + [dma((6 * NX,))] * 4
-        + [dma((3 * NX,))] * 4
+        + [dma((3 * NX,))] * 6
         + [dma((3,))] * 2,
         compiler_params=pltpu.CompilerParams(
             collective_id=0, has_side_effects=True, vmem_limit_bytes=60 << 20

time: 135 us -> 128 us (0.948)
  Pallas kernels: 134 us -> 127 us
    pallas_call x1, Pallas kernels: 131 us -> 124 us  [on_device(): pl.pallas_call(kernel, out_shape=(x_grad, jax.ShapeDtypeStruct(thirds, F3...]
where the time goes in v5:
time: 128 us
  Pallas kernels  127 us (99%)
    pallas_call x1, Pallas kernels, on_device(): pl.pallas_call(kernel, out_shape=(x_grad, jax.ShapeDtypeStruct(thirds, F3...  124 us
    pallas_call x1, Pallas kernels, on_device(): pl.pallas_call(finish, out_shape=(x_grad, grad, grad, grad), in_specs=[an...  3.16 us

profile of v5, /device:TPU:1, one launch (start us, length us, event | category | flops | bytes accessed | tf_op | source)
XLA Modules:
  0.0 127.7 jit_solution(10949979118429873876)
XLA Ops:
  0.6 123.7 %shard_map.120 = (bf16[128,2048]{1,0:T(8,128)(2,1)}, f32[3,256,768]{2,1,0:T(8,128)}, bf16[3,256,768]{2,1,0:T(8,128)(2,1)}) custom-call(s32[8,128]{1,0:T(8,128)} %bitcast.5, bf16[8,128]{1,0:T(8,128)(2,1)} %bitcast.6, s32[1,640]{1,0:T(1,128)} %constant.10.tgt_ref.inv_ref, s32[1,640]{1,0:T(1,128)} %constant.10.tgt_ref.inv_ref, bf16[128,2048]{1,0:T(8,128)(2,1)} %x_ref.1, ...), custom_call_target="tpu_custom_call" | custom-call | tf_op jit(solution)/shard_map/pallas_call | solution.py:430
  124.4 3.2 %shard_map.121 = (bf16[128,2048]{1,0:T(8,128)(2,1)}, f32[256,768]{1,0:T(8,128)}, f32[256,768]{1,0:T(8,128)}, f32[256,768]{1,0:T(8,128)}) custom-call(bf16[128,2048]{1,0:T(8,128)(2,1)} %get-tuple-element.11.xg_in, f32[3,256,768]{2,1,0:T(8,128)} %get-tuple-element.12.own_in, bf16[3,256,768]{2,1,0:T(8,128)(2,1)} %get-tuple-element.13.got_in), custom_call_target="tpu_custom_call" | custom-call | tf_op jit(solution)/shard_map/pallas_call | solution.py:482
